TPU v7x, 32 devices: a whole 2x2x4 slice. The times are simulated.
32 devices in a mesh: grp: 4 (over y, core), row: 8 (over z, x).
Axes of the slice: x: 2, y: 2, z: 4, core: 2. Of those that a mesh axis runs over, the one named last changes fastest.
Arguments:
- landmarks: bfloat16 [1024, 1024], P(('grp', 'row')), may hold values from -6.5 to 6.5
- initial_basis: bfloat16 [1024, 256], P(('grp', 'row')), may hold values from -0.1875 to 0.1875
- points: bfloat16 [32768, 1024], P(('grp', 'row')), may hold values from -6.5 to 6.5
Outputs:
- basis: float32 [1024, 256], P(('grp', 'row'))
- coords: float32 [32768, 256], P(('grp', 'row'))
All inputs are finite; a program needn't handle non-finite values.
Results may differ from a plain program's by a relative error of at most 0.0057.
Values may be sent and summed in bfloat16 or wider, within the bound.
No kernel may reach another device: no remote copies, remote signals or barrier semaphores. Data moves between devices by JAX's collectives and lax.ppermute only.
A program may use at most 128 MiB of HBM per device.

v0:
```python
import math
import jax
import jax.numpy as jnp
from jax import lax
from jax.sharding import PartitionSpec as P

ITERS = 2
spread = 0.25


def squared_rows(rows):
    return jnp.sum(jnp.square(rows.astype(jnp.float32)), axis=1)


def pair_kernel(left, right):
    inner = lax.dot_general(
        left, right, (((1,), (1,)), ((), ())), preferred_element_type=jnp.float32
    )
    dist = squared_rows(left)[:, None] + squared_rows(right)[None, :] - 2.0 * inner
    return jnp.exp(-dist / (spread * left.shape[1]))


def point_terms(anchors, spectral_rows, members, member_sq):
    inner = lax.dot_general(
        anchors, members, (((1,), (1,)), ((), ())), preferred_element_type=jnp.float32
    )
    dist = squared_rows(anchors)[:, None] + member_sq[None, :] - 2.0 * inner
    kernel_part = jnp.exp(-dist / (spread * anchors.shape[1]))
    degree_part = jnp.sum(kernel_part, axis=0)
    numer_part = lax.dot_general(
        kernel_part.astype(jnp.bfloat16),
        spectral_rows,
        (((0,), (0,)), ((), ())),
        preferred_element_type=jnp.float32,
    )
    return (numer_part, degree_part)


def body(landmarks, initial_basis, points):
    local_rows = landmarks.shape[0]
    total = local_rows * lax.axis_size("grp") * lax.axis_size("row")
    row_index = lax.axis_index("row")
    group_rows = lax.all_gather(landmarks, "row", axis=0, tiled=True)
    cross_rows = lax.all_gather(landmarks, "grp", axis=0, tiled=True)
    land_kernel = pair_kernel(group_rows, cross_rows)
    group_degree = lax.psum(jnp.sum(land_kernel, axis=1), "row")
    own_degree = lax.dynamic_slice_in_dim(group_degree, row_index * local_rows, local_rows, 0)
    cross_degree = lax.psum(jnp.sum(land_kernel, axis=0), "grp")
    row_scale = 1.0 / jnp.sqrt(group_degree)
    column_scale = 1.0 / jnp.sqrt(cross_degree)
    affinity = (land_kernel * row_scale[:, None] * column_scale[None, :]).astype(jnp.bfloat16)
    current = initial_basis
    for step in range(ITERS):
        cross_basis = lax.all_gather(current, "grp", axis=0, tiled=True)
        image = lax.psum_scatter(
            jnp.dot(affinity, cross_basis, preferred_element_type=jnp.float32),
            "row",
            scatter_dimension=0,
            tiled=True,
        )
        gram = lax.psum(jnp.dot(image.T, image, precision=lax.Precision.HIGHEST), ("grp", "row"))
        lower = jnp.linalg.cholesky(gram)
        ortho = jax.scipy.linalg.solve_triangular(lower, image.T, lower=True).T
        current = ortho.astype(jnp.bfloat16)
    lam = jnp.diagonal(lower)
    own_scale = 1.0 / jnp.sqrt(own_degree)
    spectral = (ortho * own_scale[:, None] / lam[None, :]).astype(jnp.bfloat16)
    point_sq = squared_rows(points)
    numer_part, degree_part = point_terms(
        lax.all_gather(landmarks, ("grp", "row"), axis=0, tiled=True),
        lax.all_gather(spectral, ("grp", "row"), axis=0, tiled=True),
        points,
        point_sq,
    )
    coords = numer_part / jnp.sqrt(degree_part)[:, None] * math.sqrt(total)
    return (ortho, coords)


def solution(mesh):
    in_specs = (P(("grp", "row"), None), P(("grp", "row"), None), P(("grp", "row"), None))
    out_specs = (P(("grp", "row"), None), P(("grp", "row"), None))
    return jax.shard_map(body, mesh=mesh, in_specs=in_specs, out_specs=out_specs, check_vma=False)
```

profile of v0, /device:TPU:0, one launch (start us, length us, event | category | flops | bytes accessed | tf_op | source)
XLA Modules:
  0.0 683.4 jit_solution(5649184369802876398)
XLA Ops:
  7.2 7.5 %all_gather.19 = bf16[128,1024]{1,0:T(8,128)(2,1)S(1)} all-gather(bf16[32,1024]{1,0:T(8,128)(2,1)} %param.6), channel_id=1, replica_groups=mesh['grp'=4,'row'=8] {'grp'}, dimensions={0}, use_global_device_ids=true | all-gather | bytes 327680 | tf_op jit(solution)/shard_map/all_gather | solution.py:44
  14.7 32.1 %all_gather.18 = bf16[256,1024]{1,0:T(8,128)(2,1)S(1)} all-gather(bf16[32,1024]{1,0:T(8,128)(2,1)} %param.6), channel_id=1, replica_groups=mesh['grp'=4,'row'=8] {'row'}, dimensions={0}, use_global_device_ids=true | all-gather | bytes 589824 | tf_op jit(solution)/shard_map/all_gather | solution.py:43
  46.7 5.4 all_gather.20
  52.9 21.4 %psum.28 = f32[256]{0:T(256)S(1)} all-reduce(f32[256]{0:T(256)S(1)} %get-tuple-element.20), channel_id=1, replica_groups=mesh['grp'=4,'row'=8] {'row'}, use_global_device_ids=true, to_apply=%region_3.0 | all-reduce | flops 256 | bytes 2048 | tf_op jit(solution)/shard_map/psum | solution.py:46
  74.3 5.7 psum.29
  80.9 59.6 %reduce-scatter.3.cloned.1.call-done = f32[32,256]{1,0:T(8,128)} async-done(((f32[256,256]{1,0:T(8,128)}), f32[32,256]{1,0:T(8,128)}) %reduce-scatter.3.cloned.1.call-update) | async-done | bytes 32784 | tf_op jit(solution)/shard_map/reduce_scatter | solution.py:55
  142.6 129.7 %all-reduce.4.cloned.1.call-done = f32[256,256]{0,1:T(8,128)} async-done(((f32[256,256]{0,1:T(8,128)}), f32[256,256]{0,1:T(8,128)}) %all-reduce.4.cloned.1.call-update) | async-done | bytes 262160 | tf_op jit(solution)/shard_map/psum | solution.py:61
  274.4 11.7 %cholesky.130 = f32[128,128]{1,0:T(8,128)S(1)} custom-call(f32[128,128]{1,0:T(8,128)S(1)} %cholesky.194), custom_call_target="Cholesky" | custom-call | tf_op jit(solution)/shard_map/jit(cholesky)/cholesky | solution.py:62
  286.2 9.8 %custom-call.15 = f32[1,128,128]{1,2,0:T(8,128)S(1)} custom-call(f32[1,128,128]{2,1,0:T(8,128)S(1)} %get-tuple-element.53), custom_call_target="InvertDiagBlocksLowerTriangular" | custom-call | tf_op jit(solution)/shard_map/jit(cholesky)/cholesky | solution.py:62
  296.5 11.7 %cholesky.147 = f32[128,128]{1,0:T(8,128)S(1)} custom-call(f32[128,128]{1,0:T(8,128)S(1)} %convolution_subtract_fusion.1), custom_call_target="Cholesky" | custom-call | tf_op jit(solution)/shard_map/jit(cholesky)/cholesky | solution.py:62
  310.4 4.3 while.4
  314.7 19.7 %custom-call.16 = f32[2,128,128]{1,2,0:T(8,128)S(1)} custom-call(f32[2,128,128]{2,1,0:T(8,128)S(1)} %get-tuple-element.18), custom_call_target="InvertDiagBlocksLowerTriangular" | custom-call | tf_op jit(solution)/shard_map/jit(_solve_triangular)/triangular_solve | solution.py:63
  335.0 5.2 all_gather.21
  341.3 61.2 %reduce-scatter.5.cloned.1.call-done = f32[32,256]{1,0:T(8,128)} async-done(((f32[256,256]{1,0:T(8,128)}), f32[32,256]{1,0:T(8,128)}) %reduce-scatter.5.cloned.1.call-update) | async-done | bytes 32784 | tf_op jit(solution)/shard_map/reduce_scatter | solution.py:55
  405.7 128.4 %all-reduce.6.cloned.1.call-done = f32[256,256]{0,1:T(8,128)} async-done(((f32[256,256]{0,1:T(8,128)}), f32[256,256]{0,1:T(8,128)}) %all-reduce.6.cloned.1.call-update) | async-done | bytes 262160 | tf_op jit(solution)/shard_map/psum | solution.py:61
  536.1 11.7 %cholesky.164 = f32[128,128]{1,0:T(8,128)S(1)} custom-call(f32[128,128]{1,0:T(8,128)S(1)} %cholesky.197), custom_call_target="Cholesky" | custom-call | tf_op jit(solution)/shard_map/jit(cholesky)/cholesky | solution.py:62
  547.9 9.8 %custom-call.17 = f32[1,128,128]{1,2,0:T(8,128)S(1)} custom-call(f32[1,128,128]{2,1,0:T(8,128)S(1)} %get-tuple-element.49), custom_call_target="InvertDiagBlocksLowerTriangular" | custom-call | tf_op jit(solution)/shard_map/jit(cholesky)/cholesky | solution.py:62
  558.2 11.7 %cholesky.181 = f32[128,128]{1,0:T(8,128)S(1)} custom-call(f32[128,128]{1,0:T(8,128)S(1)} %convolution_subtract_fusion), custom_call_target="Cholesky" | custom-call | tf_op jit(solution)/shard_map/jit(cholesky)/cholesky | solution.py:62
  572.6 4.2 while.5
  576.8 19.7 %custom-call.18 = f32[2,128,128]{1,2,0:T(8,128)S(1)} custom-call(f32[2,128,128]{2,1,0:T(8,128)S(1)} %get-tuple-element.19), custom_call_target="InvertDiagBlocksLowerTriangular" | custom-call | tf_op jit(solution)/shard_map/jit(_solve_triangular)/triangular_solve | solution.py:63
  596.4 2.3 gather_fusion
  600.0 68.2 %all_gather.23 = bf16[1024,256]{1,0:T(8,128)(2,1)S(1)} all-gather(bf16[32,256]{1,0:T(8,128)(2,1)S(1)} %get-tuple-element.38), channel_id=1, replica_groups=mesh['grp'=4,'row'=8] {'grp','row'}, dimensions={0}, use_global_device_ids=true | all-gather | bytes 540672 | tf_op jit(solution)/shard_map/all_gather | solution.py:71
  670.3 4.3 fusion
  674.6 2.3 divide_multiply_fusion
  (76 shorter events, 27.1 us)
Async XLA Ops:
  7.2 133.4 %reduce-scatter.3.cloned.1.call-start = ((), (), s32[]{:S(2)}) async-start(), calls=%async_computation.2 | async-start | bytes 294912 | tf_op jit(solution)/shard_map/reduce_scatter | solution.py:55
  52.5 352.7 %copy-start = (bf16[1024,1024]{1,0:T(8,128)(2,1)S(1)}, bf16[1024,1024]{1,0:T(8,128)(2,1)}, u32[]{:S(2)}) copy-start(bf16[1024,1024]{1,0:T(8,128)(2,1)} %param.8) | copy-start | bytes 6291460
  80.9 191.5 %all-reduce.4.cloned.1.call-start = ((), (), s32[]{:S(2)}) async-start(), calls=%async_computation.3 | async-start | bytes 524288 | tf_op jit(solution)/shard_map/psum | solution.py:61
  140.6 193.8 %copy-start.2 = (f32[32,256]{1,0:T(8,128)S(1)}, f32[32,256]{1,0:T(8,128)}, u32[]{:S(2)}) copy-start(f32[32,256]{1,0:T(8,128)} %reduce-scatter.3.cloned.1.call-done) | copy-start | bytes 98308
  142.6 259.9 %reduce-scatter.5.cloned.1.call-start = ((), (), s32[]{:S(2)}) async-start(), calls=%async_computation.4 | async-start | bytes 294912 | tf_op jit(solution)/shard_map/reduce_scatter | solution.py:55
  341.2 192.9 %all-reduce.6.cloned.1.call-start = ((), (), s32[]{:S(2)}) async-start(), calls=%async_computation.5 | async-start | bytes 524288 | tf_op jit(solution)/shard_map/psum | solution.py:61
  402.5 196.3 %copy-start.1 = (f32[32,256]{1,0:T(8,128)S(1)}, f32[32,256]{1,0:T(8,128)}, u32[]{:S(2)}) copy-start(f32[32,256]{1,0:T(8,128)} %reduce-scatter.5.cloned.1.call-done) | copy-start | bytes 98308
  404.5 263.7 %all-gather.2.cloned.1.call-start = ((), (), s32[]{:S(2)}) async-start(), calls=%async_computation.6 | async-start | bytes 2162688 | tf_op jit(solution)/shard_map/all_gather | solution.py:70
Sparse Core Ops, SparseCore 0:
  81.0 59.5 reduce-scatter.2
  146.7 125.6 all-reduce.3
  341.3 61.1 reduce-scatter.4
  408.4 125.5 all-reduce.5
  536.9 56.1 all-gather.1
where the time goes:
time: 684 us; the launch traced here: 683 us
  waiting for transfers between devices  380 us (56%)
  blocking collectives  145 us (21%)
  other arithmetic  114 us (17%)
  between operations  16.7 us (2%)
  matrix products  14.9 us (2%)
  local copies, waits for them, and re-layouts  12.7 us (2%)
    psum x2, waiting for transfers between devices, body(): lax.psum(jnp.dot(image.T, image, precision=lax.Precision.HIGHEST), ('grp'...  258 us
    reduce_scatter x2, waiting for transfers between devices, body(): lax.psum_scatter(jnp.dot(affinity, cross_basis, preferred_element_type=jn...  121 us
    another operation x13, other arithmetic, body(): lower = jnp.linalg.cholesky(gram)  68.6 us
    all_gather x1, blocking collectives, body(): lax.all_gather(spectral, ('grp', 'row'), axis=0, tiled=True)  68.2 us
    another operation x5, other arithmetic, body(): ortho = jax.scipy.linalg.solve_triangular(lower, image.T, lower=True).T  39.4 us
    all_gather x1, blocking collectives, body(): group_rows = lax.all_gather(landmarks, 'row', axis=0, tiled=True)  32.1 us
    psum x1, blocking collectives, body(): group_degree = lax.psum(jnp.sum(land_kernel, axis=1), 'row')  21.4 us
  transfers between devices with their start and end apart: 5, of which 4 were waited for; matrix products, arithmetic and copies ran while one was open for 9% of the time, Pallas kernels for 0%

commit v1 on v0

--- a/solution.py
+++ b/solution.py
@@ -6,6 +6,12 @@
 
 ITERS = 2
 spread = 0.25
+
+
+def gather_and_add(shard, name):
+    parts = lax.all_gather(shard, name, axis=0, tiled=False)
+    acc = parts.sum(axis=0)
+    return acc
 
 
 def squared_rows(rows):
@@ -58,7 +64,9 @@
             scatter_dimension=0,
             tiled=True,
         )
-        gram = lax.psum(jnp.dot(image.T, image, precision=lax.Precision.HIGHEST), ("grp", "row"))
+        gram = gather_and_add(
+            jnp.dot(image.T, image, precision=lax.Precision.HIGHEST), ("grp", "row")
+        )
         lower = jnp.linalg.cholesky(gram)
         ortho = jax.scipy.linalg.solve_triangular(lower, image.T, lower=True).T
         current = ortho.astype(jnp.bfloat16)

time: 684 us -> 638 us (0.933)
  waiting for transfers between devices: 380 us -> 325 us
    psum x2 -> x0, waiting for transfers between devices: 258 us -> none  [body(): lax.psum(jnp.dot(image.T, image, precision=lax.Precision.HIGHEST), ('grp'...]
    all_gather x0 -> x2, waiting for transfers between devices: none -> 149 us  [gather_and_add(): parts = lax.all_gather(shard, name, axis=0, tiled=False)]
    all_gather x1, waiting for transfers between devices: 0.01 us -> 55.8 us  [body(): lax.all_gather(landmarks, ('grp', 'row'), axis=0, tiled=True)]
    reduce_sum x0 -> x2, other arithmetic: none -> 7.86 us  [gather_and_add(): acc = parts.sum(axis=0)]
  transfers between devices with their start and end apart: 5 -> 5, of which waited for: 4 -> 5; matrix products, arithmetic and copies ran while one was open for 9% -> 2% of each run, Pallas kernels for 0% -> 0%
where the time goes in v1:
time: 638 us; the launch traced here: 637 us
  waiting for transfers between devices  325 us (51%)
  blocking collectives  146 us (23%)
  other arithmetic  120 us (19%)
  matrix products  18.8 us (3%)
  between operations  16.7 us (3%)
  local copies, waits for them, and re-layouts  10.8 us (2%)
    all_gather x2, waiting for transfers between devices, gather_and_add(): parts = lax.all_gather(shard, name, axis=0, tiled=False)  149 us
    reduce_scatter x2, waiting for transfers between devices, body(): lax.psum_scatter(jnp.dot(affinity, cross_basis, preferred_element_type=jn...  120 us
    all_gather x1, blocking collectives, body(): lax.all_gather(spectral, ('grp', 'row'), axis=0, tiled=True)  69 us
    another operation x13, other arithmetic, body(): lower = jnp.linalg.cholesky(gram)  68.8 us
    all_gather x1, waiting for transfers between devices, body(): lax.all_gather(landmarks, ('grp', 'row'), axis=0, tiled=True)  55.8 us
    another operation x5, other arithmetic, body(): ortho = jax.scipy.linalg.solve_triangular(lower, image.T, lower=True).T  39.4 us
    all_gather x1, blocking collectives, body(): group_rows = lax.all_gather(landmarks, 'row', axis=0, tiled=True)  33.3 us
    psum x1, blocking collectives, body(): group_degree = lax.psum(jnp.sum(land_kernel, axis=1), 'row')  21.5 us
  transfers between devices with their start and end apart: 5, of which 5 were waited for; matrix products, arithmetic and copies ran while one was open for 2% of the time, Pallas kernels for 0%

profile of v1, /device:TPU:0, one launch (start us, length us, event | category | flops | bytes accessed | tf_op | source)
XLA Modules:
  0.0 637.4 jit_solution(257580165895405580)
XLA Ops:
  7.2 33.3 %all_gather.30 = bf16[256,1024]{1,0:T(8,128)(2,1)S(1)} all-gather(bf16[32,1024]{1,0:T(8,128)(2,1)} %param.6), channel_id=1, replica_groups=mesh['grp'=4,'row'=8] {'row'}, dimensions={0}, use_global_device_ids=true | all-gather | bytes 589824 | tf_op jit(solution)/shard_map/all_gather | solution.py:49
  40.5 6.0 all_gather.31
  47.2 21.5 %psum.14 = f32[256]{0:T(256)S(1)} all-reduce(f32[256]{0:T(256)S(1)} %get-tuple-element.20), channel_id=1, replica_groups=mesh['grp'=4,'row'=8] {'row'}, use_global_device_ids=true, to_apply=%region_3.0 | all-reduce | flops 256 | bytes 2048 | tf_op jit(solution)/shard_map/psum | solution.py:52
  68.6 5.7 psum.15
  74.3 5.4 all_gather.32
  80.7 59.7 %reduce-scatter.3.cloned.1.call-done = f32[32,256]{1,0:T(8,128)} async-done(((f32[256,256]{1,0:T(8,128)}), f32[32,256]{1,0:T(8,128)}) %reduce-scatter.3.cloned.1.call-update) | async-done | bytes 32784 | tf_op jit(solution)/shard_map/reduce_scatter | solution.py:61
  142.4 77.7 %all-gather.8.cloned.1.call-done = f32[8192,256]{1,0:T(8,128)} async-done(((f32[256,256]{1,0:T(8,128)}), f32[8192,256]{1,0:T(8,128)}) %all-gather.8.cloned.1.call-update) | async-done | bytes 8388624 | tf_op jit(solution)/shard_map/all_gather | solution.py:12
  220.1 3.9 reduce_sum.85
  224.3 11.7 %cholesky.130 = f32[128,128]{1,0:T(8,128)S(1)} custom-call(f32[128,128]{1,0:T(8,128)S(1)} %cholesky.194), custom_call_target="Cholesky" | custom-call | tf_op jit(solution)/shard_map/jit(cholesky)/cholesky | solution.py:70
  236.0 9.8 %custom-call.15 = f32[1,128,128]{1,2,0:T(8,128)S(1)} custom-call(f32[1,128,128]{2,1,0:T(8,128)S(1)} %get-tuple-element.53), custom_call_target="InvertDiagBlocksLowerTriangular" | custom-call | tf_op jit(solution)/shard_map/jit(cholesky)/cholesky | solution.py:70
  246.3 11.7 %cholesky.147 = f32[128,128]{1,0:T(8,128)S(1)} custom-call(f32[128,128]{1,0:T(8,128)S(1)} %convolution_subtract_fusion.1), custom_call_target="Cholesky" | custom-call | tf_op jit(solution)/shard_map/jit(cholesky)/cholesky | solution.py:70
  260.3 4.3 while.4
  264.6 19.7 %custom-call.16 = f32[2,128,128]{1,2,0:T(8,128)S(1)} custom-call(f32[2,128,128]{2,1,0:T(8,128)S(1)} %get-tuple-element.18), custom_call_target="InvertDiagBlocksLowerTriangular" | custom-call | tf_op jit(solution)/shard_map/jit(_solve_triangular)/triangular_solve | solution.py:71
  284.9 5.2 all_gather.35
  291.7 60.2 %reduce-scatter.5.cloned.1.call-done = f32[32,256]{1,0:T(8,128)} async-done(((f32[256,256]{1,0:T(8,128)}), f32[32,256]{1,0:T(8,128)}) %reduce-scatter.5.cloned.1.call-update) | async-done | bytes 32784 | tf_op jit(solution)/shard_map/reduce_scatter | solution.py:61
  354.5 55.8 %all-gather.6.cloned.1.call-done = bf16[1024,1024]{1,0:T(8,128)(2,1)} async-done(((bf16[32,1024]{1,0:T(8,128)(2,1)}), bf16[1024,1024]{1,0:T(8,128)(2,1)}) %all-gather.6.cloned.1.call-update) | async-done | bytes 2097168 | tf_op jit(solution)/shard_map/all_gather | solution.py:78
  412.3 6.2 fusion
  418.5 71.1 %all-gather.10.cloned.1.call-done = f32[8192,256]{1,0:T(8,128)} async-done(((f32[256,256]{1,0:T(8,128)}), f32[8192,256]{1,0:T(8,128)}) %all-gather.10.cloned.1.call-update) | async-done | bytes 8388624 | tf_op jit(solution)/shard_map/all_gather | solution.py:12
  493.7 11.7 %cholesky.164 = f32[128,128]{1,0:T(8,128)S(1)} custom-call(f32[128,128]{1,0:T(8,128)S(1)} %cholesky.197), custom_call_target="Cholesky" | custom-call | tf_op jit(solution)/shard_map/jit(cholesky)/cholesky | solution.py:70
  505.5 9.8 %custom-call.17 = f32[1,128,128]{1,2,0:T(8,128)S(1)} custom-call(f32[1,128,128]{2,1,0:T(8,128)S(1)} %get-tuple-element.49), custom_call_target="InvertDiagBlocksLowerTriangular" | custom-call | tf_op jit(solution)/shard_map/jit(cholesky)/cholesky | solution.py:70
  515.8 11.9 %cholesky.181 = f32[128,128]{1,0:T(8,128)S(1)} custom-call(f32[128,128]{1,0:T(8,128)S(1)} %convolution_subtract_fusion), custom_call_target="Cholesky" | custom-call | tf_op jit(solution)/shard_map/jit(cholesky)/cholesky | solution.py:70
  534.3 19.7 %custom-call.18 = f32[2,128,128]{1,2,0:T(8,128)S(1)} custom-call(f32[2,128,128]{2,1,0:T(8,128)S(1)} %get-tuple-element.19), custom_call_target="InvertDiagBlocksLowerTriangular" | custom-call | tf_op jit(solution)/shard_map/jit(_solve_triangular)/triangular_solve | solution.py:71
  557.5 69.0 %all_gather.39 = bf16[1024,256]{1,0:T(8,128)(2,1)S(1)} all-gather(bf16[32,256]{1,0:T(8,128)(2,1)S(1)} %get-tuple-element.38), channel_id=1, replica_groups=mesh['grp'=4,'row'=8] {'grp','row'}, dimensions={0}, use_global_device_ids=true | all-gather | bytes 540672 | tf_op jit(solution)/shard_map/all_gather | solution.py:79
  626.5 4.4 divide_multiply_fusion
  (78 shorter events, 33.4 us)
Async XLA Ops:
  7.2 133.2 %reduce-scatter.3.cloned.1.call-start = ((), (), s32[]{:S(2)}) async-start(), calls=%async_computation.2 | async-start | bytes 294912 | tf_op jit(solution)/shard_map/reduce_scatter | solution.py:61
  80.7 139.4 %all-gather.8.cloned.1.call-start = ((), (), s32[]{:S(2)}) async-start(), calls=%async_computation.5 | async-start | bytes 8650752 | tf_op jit(solution)/shard_map/all_gather | solution.py:12
  142.4 209.5 %reduce-scatter.5.cloned.1.call-start = ((), (), s32[]{:S(2)}) async-start(), calls=%async_computation.3 | async-start | bytes 294912 | tf_op jit(solution)/shard_map/reduce_scatter | solution.py:61
  220.1 64.1 %copy-start.2 = (f32[32,256]{1,0:T(8,128)S(1)}, f32[32,256]{1,0:T(8,128)}, u32[]{:S(2)}) copy-start(f32[32,256]{1,0:T(8,128)} %reduce-scatter.3.cloned.1.call-done) | copy-start | bytes 98308
  224.1 129.9 %copy-start = (bf16[1024,1024]{1,0:T(8,128)(2,1)S(1)}, bf16[1024,1024]{1,0:T(8,128)(2,1)}, u32[]{:S(2)}) copy-start(bf16[1024,1024]{1,0:T(8,128)(2,1)} %param.8) | copy-start | bytes 6291460
  291.1 119.2 %all-gather.6.cloned.1.call-start = ((), (), s32[]{:S(2)}) async-start(), calls=%async_computation.4 | async-start | bytes 2162688 | tf_op jit(solution)/shard_map/all_gather | solution.py:78
  291.6 198.0 %all-gather.10.cloned.1.call-start = ((), (), s32[]{:S(2)}) async-start(), calls=%async_computation.6 | async-start | bytes 8650752 | tf_op jit(solution)/shard_map/all_gather | solution.py:12
  493.5 60.5 %copy-start.1 = (f32[32,256]{1,0:T(8,128)S(1)}, f32[32,256]{1,0:T(8,128)}, u32[]{:S(2)}) copy-start(f32[32,256]{1,0:T(8,128)} %reduce-scatter.5.cloned.1.call-done) | copy-start | bytes 98308
Sparse Core Ops, SparseCore 0:
  80.8 59.5 reduce-scatter.2
  144.0 76.1 all-gather.7
  291.2 60.6 reduce-scatter.4
  354.7 55.4 all-gather.5
  413.6 75.9 all-gather.9
